TPU v7x, 32 devices: a whole 2x2x4 slice. The times are simulated.
32 devices in a mesh: sector: 8 (over z, y), term: 4 (over x, core).
Axes of the slice: x: 2, y: 2, z: 4, core: 2. Of those that a mesh axis runs over, the one named last changes fastest.
Arguments:
- trial_vector: bfloat16 [8, 512, 512], P('sector'), may hold values from -6 to 6
- sector_energy: float32 [8], P('sector'), may hold values from 0.5 to 4
- left_blocks: bfloat16 [64, 8, 512, 512], P('term', 'sector'), may hold values from -0.25 to 0.25
- right_blocks: bfloat16 [64, 8, 512, 512], P('term', 'sector'), may hold values from -0.046875 to 0.046875
- source_sector: int32 [64, 8], P('term', 'sector'), may hold values from 0 to 7
- coupled: int32 [64, 8], P('term', 'sector'), may hold values from 0 to 1, as said below
Outputs:
- applied: float32 [8, 512, 512], P('sector', 'term')
- ritz_values: float32 [2], replicated
Inputs may be any that keep to these rules, and one draw needn't show every extreme that they name: Each target sector has its own density of coupled terms.
All inputs are finite; a program needn't handle non-finite values.
Results may differ from a plain program's by a relative error of at most 0.004.
Values may be sent and summed in bfloat16 or wider, within the bound.
A program may use at most 64 MiB of HBM per device.

v0:
```python
import jax
import jax.numpy as jnp
from jax import lax
from jax.sharding import PartitionSpec as P


def body(trial_vector, sector_energy, left_blocks, right_blocks, source_sector, coupled):
    term_count = left_blocks.shape[0]
    sector_local = left_blocks.shape[1]
    order = left_blocks.shape[2]
    pairs = term_count * sector_local

    def add_block(carry, blocks, index, term_idx, sector_idx):
        block = lax.dynamic_index_in_dim(blocks, index, 0, keepdims=False)
        middle = jnp.dot(
            left_blocks[term_idx, sector_idx], block, preferred_element_type=jnp.float32
        ).astype(jnp.bfloat16)
        product = jnp.dot(
            middle, right_blocks[term_idx, sector_idx], preferred_element_type=jnp.float32
        )
        return carry.at[sector_idx].add(product)

    def apply_terms(vector_own):
        empty = jnp.zeros((sector_local, order, order), jnp.float32)
        whole = lax.all_gather(vector_own, "sector", axis=0, tiled=True)

        def step(pair, total):
            term_idx = pair // sector_local
            sector_idx = pair % sector_local
            return lax.cond(
                coupled[term_idx, sector_idx] > 0,
                lambda carry: add_block(
                    carry, whole, source_sector[term_idx, sector_idx], term_idx, sector_idx
                ),
                lambda carry: carry,
                total,
            )

        return lax.fori_loop(0, pairs, step, empty)

    entries = float(sector_local * lax.axis_size("sector") * order * order)
    energy_col = sector_energy[:, None, None]
    share_rows = order // lax.axis_size("term")
    row_start = lax.axis_index("term") * share_rows
    partial_first = apply_terms(trial_vector)
    trial = trial_vector.astype(jnp.float32)
    first = lax.psum(partial_first, "term") + energy_col * trial
    cross, square = lax.psum((jnp.sum(trial * first), jnp.sum(trial * trial)), "sector")
    rayleigh = cross / square
    residual = first - rayleigh * trial
    total_sq = lax.psum(jnp.sum(residual * residual), "sector")
    vector_rms = jnp.sqrt(total_sq / entries + 1e-06)
    next_vector = (residual / vector_rms).astype(jnp.bfloat16)
    partial_second = apply_terms(next_vector)
    next_rows_f = lax.dynamic_slice_in_dim(next_vector, row_start, share_rows, 1).astype(
        jnp.float32
    )
    applied = (
        lax.psum_scatter(partial_second, "term", scatter_dimension=1, tiled=True)
        + energy_col * next_rows_f
    )
    return (applied, jnp.stack([rayleigh, vector_rms]))


def solution(mesh):
    return jax.shard_map(
        body,
        mesh=mesh,
        in_specs=(
            P("sector", None, None),
            P("sector"),
            P("term", "sector", None, None),
            P("term", "sector", None, None),
            P("term", "sector"),
            P("term", "sector"),
        ),
        out_specs=(P("sector", "term", None), P()),
        check_vma=False,
    )
```

profile of v0, /device:TPU:0, one launch (start us, length us, event | category | flops | bytes accessed | tf_op | source)
XLA Modules:
  0.0 504.4 jit_solution(15628373344778372390)
XLA Ops:
  7.9 78.3 %all-gather.3.cloned.1.call-done = bf16[8,512,512]{2,1,0:T(8,128)(2,1)} async-done(((bf16[1,512,512]{2,1,0:T(8,128)(2,1)}), bf16[8,512,512]{2,1,0:T(8,128)(2,1)}) %all-gather.3.cloned.1.call-update) | async-done | bytes 4194320 | tf_op jit(solution)/shard_map/all_gather | solution.py:25
  86.4 68.0 %while.40 = (s32[]{:T(128)}, f32[1,512,512]{2,1,0:T(8,128)S(1)}, s32[16,1]{0,1:T(1,128)}, bf16[16,1,512,512]{3,2,1,0:T(8,128)(2,1)}, s32[16,1]{0,1:T(1,128)}, /*...) while((s32[]{:T(128)}, f32[1,512,512]{2,1,0:T(8,128)S(1)}, ...), condition=%wide.region_4.5_spmd, body=%wide.region_0.4_spmd.sunk | while | flops 537395200 | bytes 3671787 | solution.py:39
  86.4 1.3 fusion.34
  90.3 5.3 %conditional.4 = (f32[1,512,512]{2,1,0:T(8,128)S(1)}) conditional(s32[]{:T(128)} %bitcast.39, f32[1,512,512]{2,1,0:T(8,128)S(1)} %get-tuple-element.693, (s32[]{:T(128)}, bf16[16,1,512,512]{3,2,1,0:T(8,128)(2,1)}, s32[16,1]{0,1:T(1,128)}, bf16[8,512,512]{2,1,0:T(8,128)(2,1)}, bf16[16,1,512,512]{3,2,1,0:T(8,128)(2,1)}, ...), branch_computations={%region_1.1_spmd, %region_2.3_spmd} | conditional | flops 537395200 | bytes 3671640 | solution.py:30
  93.5 2.1 fusion
  97.5 5.3 %conditional.4 = (f32[1,512,512]{2,1,0:T(8,128)S(1)}) conditional(s32[]{:T(128)} %bitcast.39, f32[1,512,512]{2,1,0:T(8,128)S(1)} %get-tuple-element.693, (s32[]{:T(128)}, bf16[16,1,512,512]{3,2,1,0:T(8,128)(2,1)}, s32[16,1]{0,1:T(1,128)}, bf16[8,512,512]{2,1,0:T(8,128)(2,1)}, bf16[16,1,512,512]{3,2,1,0:T(8,128)(2,1)}, ...), branch_computations={%region_1.1_spmd, %region_2.3_spmd} | conditional | flops 537395200 | bytes 3671640 | solution.py:30
  100.7 2.1 fusion
  114.4 5.3 %conditional.4 = (f32[1,512,512]{2,1,0:T(8,128)S(1)}) conditional(s32[]{:T(128)} %bitcast.39, f32[1,512,512]{2,1,0:T(8,128)S(1)} %get-tuple-element.693, (s32[]{:T(128)}, bf16[16,1,512,512]{3,2,1,0:T(8,128)(2,1)}, s32[16,1]{0,1:T(1,128)}, bf16[8,512,512]{2,1,0:T(8,128)(2,1)}, bf16[16,1,512,512]{3,2,1,0:T(8,128)(2,1)}, ...), branch_computations={%region_1.1_spmd, %region_2.3_spmd} | conditional | flops 537395200 | bytes 3671640 | solution.py:30
  117.6 2.1 fusion
  123.5 5.3 %conditional.4 = (f32[1,512,512]{2,1,0:T(8,128)S(1)}) conditional(s32[]{:T(128)} %bitcast.39, f32[1,512,512]{2,1,0:T(8,128)S(1)} %get-tuple-element.693, (s32[]{:T(128)}, bf16[16,1,512,512]{3,2,1,0:T(8,128)(2,1)}, s32[16,1]{0,1:T(1,128)}, bf16[8,512,512]{2,1,0:T(8,128)(2,1)}, bf16[16,1,512,512]{3,2,1,0:T(8,128)(2,1)}, ...), branch_computations={%region_1.1_spmd, %region_2.3_spmd} | conditional | flops 537395200 | bytes 3671640 | solution.py:30
  126.8 2.1 fusion
  130.8 5.3 %conditional.4 = (f32[1,512,512]{2,1,0:T(8,128)S(1)}) conditional(s32[]{:T(128)} %bitcast.39, f32[1,512,512]{2,1,0:T(8,128)S(1)} %get-tuple-element.693, (s32[]{:T(128)}, bf16[16,1,512,512]{3,2,1,0:T(8,128)(2,1)}, s32[16,1]{0,1:T(1,128)}, bf16[8,512,512]{2,1,0:T(8,128)(2,1)}, bf16[16,1,512,512]{3,2,1,0:T(8,128)(2,1)}, ...), branch_computations={%region_1.1_spmd, %region_2.3_spmd} | conditional | flops 537395200 | bytes 3671640 | solution.py:30
  134.0 2.1 fusion
  138.0 5.3 %conditional.4 = (f32[1,512,512]{2,1,0:T(8,128)S(1)}) conditional(s32[]{:T(128)} %bitcast.39, f32[1,512,512]{2,1,0:T(8,128)S(1)} %get-tuple-element.693, (s32[]{:T(128)}, bf16[16,1,512,512]{3,2,1,0:T(8,128)(2,1)}, s32[16,1]{0,1:T(1,128)}, bf16[8,512,512]{2,1,0:T(8,128)(2,1)}, bf16[16,1,512,512]{3,2,1,0:T(8,128)(2,1)}, ...), branch_computations={%region_1.1_spmd, %region_2.3_spmd} | conditional | flops 537395200 | bytes 3671640 | solution.py:30
  141.2 2.1 fusion
  145.2 5.3 %conditional.4 = (f32[1,512,512]{2,1,0:T(8,128)S(1)}) conditional(s32[]{:T(128)} %bitcast.39, f32[1,512,512]{2,1,0:T(8,128)S(1)} %get-tuple-element.693, (s32[]{:T(128)}, bf16[16,1,512,512]{3,2,1,0:T(8,128)(2,1)}, s32[16,1]{0,1:T(1,128)}, bf16[8,512,512]{2,1,0:T(8,128)(2,1)}, bf16[16,1,512,512]{3,2,1,0:T(8,128)(2,1)}, ...), branch_computations={%region_1.1_spmd, %region_2.3_spmd} | conditional | flops 537395200 | bytes 3671640 | solution.py:30
  148.4 2.1 fusion
  156.2 80.7 %all-reduce.3.cloned.1.call-done = f32[1,512,512]{2,1,0:T(8,128)} async-done(((f32[1,512,512]{2,1,0:T(8,128)}), f32[1,512,512]{2,1,0:T(8,128)}) %all-reduce.3.cloned.1.call-update) | async-done | bytes 1048592 | tf_op jit(solution)/shard_map/psum | solution.py:47
  236.8 2.1 fusion.28
  238.9 22.0 %all-reduce = (f32[]{:T(128)}, f32[]{:T(128)}) all-reduce(f32[]{:T(128)} %get-tuple-element.567, f32[]{:T(128)} %get-tuple-element.566), channel_id=1, replica_groups=mesh['sector'=8,'term'=4] {'sector'}, use_global_device_ids=true, to_apply=%region_7.8 | all-reduce | flops 2 | bytes 16 | tf_op jit(solution)/shard_map/psum | solution.py:48
  262.3 2.1 multiply_reduce_fusion
  264.4 17.7 %psum.31 = f32[]{:T(128)} all-reduce(f32[]{:T(128)} %multiply_reduce_fusion), channel_id=1, replica_groups=mesh['sector'=8,'term'=4] {'sector'}, use_global_device_ids=true, to_apply=%region_11.12 | all-reduce | flops 1 | bytes 8 | tf_op jit(solution)/shard_map/psum | solution.py:51
  282.8 2.2 divide_convert_fusion
  285.1 71.7 %all-gather.5.cloned.1.call-done = bf16[8,512,512]{2,1,0:T(8,128)(2,1)} async-done(((bf16[1,512,512]{2,1,0:T(8,128)(2,1)}), bf16[8,512,512]{2,1,0:T(8,128)(2,1)}) %all-gather.5.cloned.1.call-update) | async-done | bytes 4194320 | tf_op jit(solution)/shard_map/all_gather | solution.py:25
  356.9 68.1 %while.41 = (s32[]{:T(128)}, f32[1,512,512]{2,1,0:T(8,128)S(1)}, s32[16,1]{0,1:T(1,128)}, bf16[16,1,512,512]{3,2,1,0:T(8,128)(2,1)}, s32[16,1]{0,1:T(1,128)}, /*...) while((s32[]{:T(128)}, f32[1,512,512]{2,1,0:T(8,128)S(1)}, ...), condition=%wide.region_16.17_spmd, body=%wide.region_12.16_spmd.sunk | while | flops 537395200 | bytes 3671787 | solution.py:39
  357.0 1.3 fusion.35
  358.9 1.3 fusion.35
  360.8 5.3 %conditional.5 = (f32[1,512,512]{2,1,0:T(8,128)S(1)}) conditional(s32[]{:T(128)} %bitcast.40, f32[1,512,512]{2,1,0:T(8,128)S(1)} %get-tuple-element.717, (s32[]{:T(128)}, bf16[16,1,512,512]{3,2,1,0:T(8,128)(2,1)}, s32[16,1]{0,1:T(1,128)}, bf16[8,512,512]{2,1,0:T(8,128)(2,1)}, bf16[16,1,512,512]{3,2,1,0:T(8,128)(2,1)}, ...), branch_computations={%region_13.13_spmd, %region_14.15_spmd} | conditional | flops 537395200 | bytes 3671640 | solution.py:30
  360.8 1.3 constant_dynamic-slice_fusion.2
  364.0 2.1 fusion.13
  366.1 1.3 fusion.35
  368.0 5.3 %conditional.5 = (f32[1,512,512]{2,1,0:T(8,128)S(1)}) conditional(s32[]{:T(128)} %bitcast.40, f32[1,512,512]{2,1,0:T(8,128)S(1)} %get-tuple-element.717, (s32[]{:T(128)}, bf16[16,1,512,512]{3,2,1,0:T(8,128)(2,1)}, s32[16,1]{0,1:T(1,128)}, bf16[8,512,512]{2,1,0:T(8,128)(2,1)}, bf16[16,1,512,512]{3,2,1,0:T(8,128)(2,1)}, ...), branch_computations={%region_13.13_spmd, %region_14.15_spmd} | conditional | flops 537395200 | bytes 3671640 | solution.py:30
  368.1 1.3 constant_dynamic-slice_fusion.2
  371.2 2.1 fusion.13
  373.4 1.3 fusion.35
  375.3 1.3 fusion.35
  377.2 1.3 fusion.35
  379.2 1.3 fusion.35
  381.1 1.3 fusion.35
  383.1 1.3 fusion.35
  385.0 5.3 %conditional.5 = (f32[1,512,512]{2,1,0:T(8,128)S(1)}) conditional(s32[]{:T(128)} %bitcast.40, f32[1,512,512]{2,1,0:T(8,128)S(1)} %get-tuple-element.717, (s32[]{:T(128)}, bf16[16,1,512,512]{3,2,1,0:T(8,128)(2,1)}, s32[16,1]{0,1:T(1,128)}, bf16[8,512,512]{2,1,0:T(8,128)(2,1)}, bf16[16,1,512,512]{3,2,1,0:T(8,128)(2,1)}, ...), branch_computations={%region_13.13_spmd, %region_14.15_spmd} | conditional | flops 537395200 | bytes 3671640 | solution.py:30
  385.0 1.3 constant_dynamic-slice_fusion.2
  388.2 2.1 fusion.13
  390.3 1.3 fusion.35
  392.2 1.3 fusion.35
  394.1 5.3 %conditional.5 = (f32[1,512,512]{2,1,0:T(8,128)S(1)}) conditional(s32[]{:T(128)} %bitcast.40, f32[1,512,512]{2,1,0:T(8,128)S(1)} %get-tuple-element.717, (s32[]{:T(128)}, bf16[16,1,512,512]{3,2,1,0:T(8,128)(2,1)}, s32[16,1]{0,1:T(1,128)}, bf16[8,512,512]{2,1,0:T(8,128)(2,1)}, bf16[16,1,512,512]{3,2,1,0:T(8,128)(2,1)}, ...), branch_computations={%region_13.13_spmd, %region_14.15_spmd} | conditional | flops 537395200 | bytes 3671640 | solution.py:30
  394.2 1.3 constant_dynamic-slice_fusion.2
  397.3 2.1 fusion.13
  399.5 1.3 fusion.35
  401.4 5.3 %conditional.5 = (f32[1,512,512]{2,1,0:T(8,128)S(1)}) conditional(s32[]{:T(128)} %bitcast.40, f32[1,512,512]{2,1,0:T(8,128)S(1)} %get-tuple-element.717, (s32[]{:T(128)}, bf16[16,1,512,512]{3,2,1,0:T(8,128)(2,1)}, s32[16,1]{0,1:T(1,128)}, bf16[8,512,512]{2,1,0:T(8,128)(2,1)}, bf16[16,1,512,512]{3,2,1,0:T(8,128)(2,1)}, ...), branch_computations={%region_13.13_spmd, %region_14.15_spmd} | conditional | flops 537395200 | bytes 3671640 | solution.py:30
  401.4 1.3 constant_dynamic-slice_fusion.2
  404.6 2.1 fusion.13
  406.7 1.3 fusion.35
  408.6 5.3 %conditional.5 = (f32[1,512,512]{2,1,0:T(8,128)S(1)}) conditional(s32[]{:T(128)} %bitcast.40, f32[1,512,512]{2,1,0:T(8,128)S(1)} %get-tuple-element.717, (s32[]{:T(128)}, bf16[16,1,512,512]{3,2,1,0:T(8,128)(2,1)}, s32[16,1]{0,1:T(1,128)}, bf16[8,512,512]{2,1,0:T(8,128)(2,1)}, bf16[16,1,512,512]{3,2,1,0:T(8,128)(2,1)}, ...), branch_computations={%region_13.13_spmd, %region_14.15_spmd} | conditional | flops 537395200 | bytes 3671640 | solution.py:30
  408.6 1.3 constant_dynamic-slice_fusion.2
  411.8 2.1 fusion.13
  413.9 1.3 fusion.35
  415.8 5.3 %conditional.5 = (f32[1,512,512]{2,1,0:T(8,128)S(1)}) conditional(s32[]{:T(128)} %bitcast.40, f32[1,512,512]{2,1,0:T(8,128)S(1)} %get-tuple-element.717, (s32[]{:T(128)}, bf16[16,1,512,512]{3,2,1,0:T(8,128)(2,1)}, s32[16,1]{0,1:T(1,128)}, bf16[8,512,512]{2,1,0:T(8,128)(2,1)}, bf16[16,1,512,512]{3,2,1,0:T(8,128)(2,1)}, ...), branch_computations={%region_13.13_spmd, %region_14.15_spmd} | conditional | flops 537395200 | bytes 3671640 | solution.py:30
  415.8 1.3 constant_dynamic-slice_fusion.2
  419.0 2.1 fusion.13
  421.1 1.3 fusion.35
  423.1 1.3 fusion.35
  426.6 69.5 %reduce-scatter.2.cloned.1.call-done = f32[1,128,512]{2,1,0:T(8,128)} async-done(((f32[1,512,512]{2,1,0:T(8,128)}), f32[1,128,512]{2,1,0:T(8,128)}) %reduce-scatter.2.cloned.1.call-update) | async-done | bytes 262160 | tf_op jit(solution)/shard_map/reduce_scatter | solution.py:59
  496.1 1.7 multiply_add_fusion
  (57 shorter events, 31.2 us)
Async XLA Ops:
  7.2 79.1 %all-gather.3.cloned.1.call-start = ((), (), s32[]{:S(2)}) async-start(), calls=%async_computation.1 | async-start | bytes 4718592 | tf_op jit(solution)/shard_map/all_gather | solution.py:25
  7.9 228.9 %all-reduce.3.cloned.1.call-start = ((), (), s32[]{:S(2)}) async-start(), calls=%async_computation.2 | async-start | bytes 2097152 | tf_op jit(solution)/shard_map/psum | solution.py:47
  86.4 150.5 %copy-start.2 = (bf16[1,512,512]{2,1,0:T(8,128)(2,1)S(1)}, bf16[1,512,512]{2,1,0:T(8,128)(2,1)}, u32[]{:S(2)}) copy-start(bf16[1,512,512]{2,1,0:T(8,128)(2,1)} %param.18) | copy-start | bytes 1572868
  154.4 1.0 copy-start.1
  155.5 201.4 %all-gather.5.cloned.1.call-start = ((), (), s32[]{:S(2)}) async-start(), calls=%async_computation.3 | async-start | bytes 4718592 | tf_op jit(solution)/shard_map/all_gather | solution.py:25
  285.1 211.1 %reduce-scatter.2.cloned.1.call-start = ((), (), s32[]{:S(2)}) async-start(), calls=%async_computation.4 | async-start | bytes 1310720 | tf_op jit(solution)/shard_map/reduce_scatter | solution.py:59
  425.0 1.0 copy-start
Sparse Core Ops, SparseCore 0:
  10.1 76.0 all-gather.2
  155.6 81.2 all-reduce.2
  285.2 71.5 all-gather.4
  426.1 69.9 reduce-scatter.1
where the time goes:
time: 507 us; the launch traced here: 504 us
  waiting for transfers between devices  301 us (59%)
  loops' own time  49 us (10%)
  other arithmetic  49 us (10%)
  blocking collectives  39.7 us (8%)
  matrix products  29.4 us (6%)
  local copies, waits for them, and re-layouts  19.7 us (4%)
  between operations  16.5 us (3%)
    all_gather x2, waiting for transfers between devices, apply_terms(): whole = lax.all_gather(vector_own, 'sector', axis=0, tiled=True)  150 us
    psum x1, waiting for transfers between devices, body(): first = lax.psum(partial_first, 'term') + energy_col * trial  80.7 us
    reduce_scatter x1, waiting for transfers between devices, body(): lax.psum_scatter(partial_second, 'term', scatter_dimension=1, tiled=True)  69.5 us
    gt x32, other arithmetic, step(): coupled[term_idx, sector_idx] > 0  40.2 us
    dot_general x14, matrix products, add_block(): jnp.dot(middle, right_blocks[term_idx, sector_idx], preferred_element_typ...  29.4 us
    another operation x32, loops' own time, step(): lax.cond(coupled[term_idx, sector_idx] > 0, lambda carry: add_block(carry...  27.6 us
    psum x1, blocking collectives, body(): lax.psum((jnp.sum(trial * first), jnp.sum(trial * trial)), 'sector')  22 us
    another operation x2, loops' own time, apply_terms(): return lax.fori_loop(0, pairs, step, empty)  21.4 us
  transfers between devices with their start and end apart: 4, of which 4 were waited for; matrix products, arithmetic and copies ran while one was open for 0% of the time, Pallas kernels for 0%

commit v1 on v0

v1 whole, which is shorter than its diff:
```python
import functools
import jax
import jax.numpy as jnp
from jax import lax
from jax.experimental import pallas as pl
from jax.experimental.pallas import tpu as pltpu
from jax.sharding import PartitionSpec as P

MESH = pl.DeviceIdType.MESH
F32 = jnp.float32
BF16 = jnp.bfloat16
CORES = 2
CHUNKS = 2


def plan(sectors, terms, order):
    na = 4 if sectors % 4 == 0 else sectors
    nb = sectors // na
    nx = terms // CORES
    share = order // terms
    early = 48 if (nx == 2 and share == 128) else 0
    return na, nb, nx, share, early


def kernel(
    sectors, terms, count, order,
    trial_ref, energy_ref, left_hbm, right_hbm, source_ref, coupled_ref,
    out_ref, ritz_ref,
    left, right, vecs, mid, acc, rs_core, rs_send, rs_x, red_term, red_sector, red_send, own,
    send_sem, recv_sem, left_sem, right_sem,
):
    na, nb, nx, share, early = plan(sectors, terms, order)
    width = order // CHUNKS
    s = lax.axis_index("sector")
    t = lax.axis_index("term")
    a, b = s // nb, lax.rem(s, nb)
    x, core = t // CORES, lax.rem(t, CORES)
    other = 1 - core

    def vec(g, c):
        return vecs[g * CHUNKS + c]

    ids = {}
    pending = []

    def sem_id(key):
        return ids.setdefault(key, len(ids))

    def send(src, dst, key, device):
        k = sem_id(key)
        copy = pltpu.make_async_remote_copy(
            src_ref=src, dst_ref=dst, send_sem=send_sem.at[k], recv_sem=recv_sem.at[k],
            device_id=device, device_id_type=MESH,
        )
        copy.start()
        pending.append(copy)

    def recv(dst, key):
        k = sem_id(key)
        pltpu.make_async_remote_copy(
            src_ref=dst, dst_ref=dst, send_sem=send_sem.at[k], recv_sem=recv_sem.at[k],
            device_id=(s, t), device_id_type=MESH,
        ).wait_recv()

    def flush():
        for copy in pending:
            copy.wait_send()
        pending.clear()

    def at_a(i):
        return (lax.rem(a + i, na) * nb + b, t)

    def at_b(j):
        return (a * nb + lax.rem(b + j, nb), t)

    def at_x(k):
        return (s, lax.rem(x + k, nx) * CORES + core)

    at_core = (s, x * CORES + other)

    def sec(i, j):
        return lax.rem(a - i + na, na) * nb + lax.rem(b - j + nb, nb)

    def quarter(k, c):
        return lax.rem(x - k + nx, nx) * CORES + c

    def rows(part, low=0, size=None):
        size = share - low if size is None else size
        return pl.ds(pl.multiple_of(part * share + low, 16), size)

    for k in range(count):
        pltpu.make_async_copy(left_hbm.at[k, 0], left.at[k], left_sem.at[k]).start()
    for k in range(count):
        pltpu.make_async_copy(right_hbm.at[k, 0], right.at[k], right_sem.at[k]).start()

    barrier = pltpu.get_barrier_semaphore()
    for k in range(1, terms):
        pl.semaphore_signal(barrier, inc=1, device_id=(s, lax.rem(t + k, terms)), device_id_type=MESH)
    for k in range(1, sectors):
        pl.semaphore_signal(barrier, inc=1, device_id=(lax.rem(s + k, sectors), t), device_id_type=MESH)
    for c in range(CHUNKS):
        vec(0, c)[s] = trial_ref[0, :, c * width:(c + 1) * width]
    pl.semaphore_wait(barrier, terms + sectors - 2)

    def gather(g, c):
        def ref(sector, where):
            return vec(g, c).at[sector, where]

        def push(sector, where, key, device):
            send(ref(sector, where), ref(sector, where), (g, c) + key, device)

        def pull(sector, where, key):
            recv(ref(sector, where), (g, c) + key)

        mine = rows(t)
        peer_early = rows(quarter(1, core), 0, early) if early else None

        def first():
            if g == 1:
                for k in range(1, nx):
                    push(s, mine, ("x0", k), at_x(k))
                push(s, mine, ("c", 0, 0, 0), at_core)
            for i in range(na - 1, 0, -1):
                push(s, mine, ("a", i), at_a(i))

        def second():
            if g == 1:
                for k in range(1, nx):
                    pull(s, rows(quarter(k, core)), ("x0", k))
            if early:
                for i in range(na - 1, 0, -1):
                    push(s, peer_early, ("aq", i), at_a(i))
            if g == 1:
                for k in range(1, nx):
                    push(s, rows(quarter(k, core)), ("c", 0, 0, k), at_core)

        def distribute(i, j):
            for k in range(1, nx):
                push(sec(i, j), rows(t, early), ("x", i, j, k), at_x(k))
            push(sec(i, j), mine, ("c", i, j, 0), at_core)

        def third():
            for i in range(na):
                if i:
                    pull(sec(i, 0), mine, ("a", i))
                    if early:
                        pull(sec(i, 0), peer_early, ("aq", i))
                for j in range(1, nb):
                    push(sec(i, 0), mine, ("b", i, j), at_b(j))
                    if early:
                        push(sec(i, 0), peer_early, ("bq", i, j), at_b(j))
                if i:
                    distribute(i, 0)

        def fourth():
            for i in range(na):
                for j in range(1, nb):
                    pull(sec(i, j), mine, ("b", i, j))
                    if early:
                        pull(sec(i, j), peer_early, ("bq", i, j))
                    distribute(i, j)

        order_of = [(i, 0) for i in range(1, na)] + [(i, j) for i in range(na) for j in range(1, nb)]

        def fifth():
            for i, j in order_of:
                for k in range(1, nx):
                    pull(sec(i, j), rows(quarter(k, core), early), ("x", i, j, k))
                    push(sec(i, j), rows(quarter(k, core)), ("c", i, j, k), at_core)

        def last():
            for i, j in ([(0, 0)] if g == 1 else []) + order_of:
                for k in range(nx):
                    pull(sec(i, j), rows(quarter(k, other)), ("c", i, j, k))

        return [first, second, third, fourth, fifth, last]

    def middles(g, c, low, high):
        def step(k, carry):
            made = jnp.dot(left[k], vec(g, c)[source_ref[k, 0]], preferred_element_type=F32)
            mid[k, :, c * width:(c + 1) * width] = jnp.where(coupled_ref[k, 0] > 0, made, 0.0).astype(BF16)
            return carry

        lax.fori_loop(low, high, step, 0)

    def products(c, low, high):
        cols = slice(c * width, (c + 1) * width)
        if low == 0:
            acc[c] = jnp.dot(mid[0], right[0, :, cols], preferred_element_type=F32)
            low = 1

        def step(k, carry):
            acc[c] += jnp.dot(mid[k], right[k, :, cols], preferred_element_type=F32)
            return carry

        lax.fori_loop(low, high, step, 0)

    def reduce_core(g, c):
        for k in range(nx):
            part = lax.rem(x + k, nx) * CORES + other
            send(acc.at[c, rows(part)], rs_core.at[c, k], ("rc", g, c, k), at_core)

    def reduce_x(g, c):
        for k in range(1, nx):
            recv(rs_core.at[c, k], ("rc", g, c, k))
            part = lax.rem(x + k, nx) * CORES + core
            rs_send[c, k - 1] = acc[c, rows(part)] + rs_core[c, k]
            send(rs_send.at[c, k - 1], rs_x.at[c, k - 1], ("rx", g, c, k), at_x(k))

    def reduce_last(g, c):
        recv(rs_core.at[c, 0], ("rc", g, c, 0))
        total = acc[c, rows(t)] + rs_core[c, 0]
        for k in range(1, nx):
            recv(rs_x.at[c, k - 1], ("rx", g, c, k))
            total = total + rs_x[c, k - 1]
        return total

    def sum_term(n, tile):
        red_send[n, 0] = tile
        red_term[n, t] = tile
        for k in range(1, terms):
            send(red_send.at[n, 0], red_term.at[n, t], ("st", n, k), (s, lax.rem(t + k, terms)))

    def sum_sector(n):
        for k in range(1, terms):
            recv(red_term.at[n, lax.rem(t - k + terms, terms)], ("st", n, k))
        tile = red_term[n, 0]
        for k in range(1, terms):
            tile = tile + red_term[n, k]
        red_send[n, 1] = tile
        red_sector[n, s] = tile
        for k in range(1, sectors):
            send(red_send.at[n, 1], red_sector.at[n, s], ("ss", n, k), (lax.rem(s + k, sectors), t))

    def sum_last(n):
        for k in range(1, sectors):
            recv(red_sector.at[n, lax.rem(s - k + sectors, sectors)], ("ss", n, k))
        tile = red_sector[n, 0]
        for k in range(1, sectors):
            tile = tile + red_sector[n, k]
        return tile

    energy = energy_ref[0]
    half = count // 2

    def application(g, between):
        steps = [gather(g, c) for c in range(CHUNKS)]
        for c in range(CHUNKS):
            steps[c][0]()
        for c in range(CHUNKS):
            steps[c][1]()
        for stage in range(2, 6):
            steps[0][stage]()
        marks = [0, count // 4, half, 3 * count // 4, count]
        for n in range(4):
            if g == 0:
                for k in range(marks[n], marks[n + 1]):
                    pltpu.make_async_copy(left_hbm.at[k, 0], left.at[k], left_sem.at[k]).wait()
            middles(g, 0, marks[n], marks[n + 1])
            steps[1][2 + n]()
        middles(g, 1, 0, count)
        if g == 0:
            for k in range(count):
                pltpu.make_async_copy(right_hbm.at[k, 0], right.at[k], right_sem.at[k]).wait()
        products(0, 0, count)
        reduce_core(g, 0)
        products(1, 0, half)
        reduce_x(g, 0)
        products(1, half, count)
        reduce_core(g, 1)
        between()
        reduce_x(g, 1)

    def trial_rows(c):
        return trial_ref[0, rows(t), c * width:(c + 1) * width].astype(F32)

    sub = lax.broadcasted_iota(jnp.int32, (8, 128), 0)

    def start_rayleigh():
        cross = F32(0.0)
        square = F32(0.0)
        for c in range(CHUNKS):
            cross += jnp.sum(acc[c] * trial_ref[0, :, c * width:(c + 1) * width].astype(F32))
            square += jnp.sum(trial_rows(c) * trial_rows(c))
        sum_term(0, jnp.where(sub == 0, cross + energy * square, square))

    application(0, start_rayleigh)
    sum_sector(0)
    for c in range(CHUNKS):
        own[c] = reduce_last(0, c) + energy * trial_rows(c)
    sums = sum_last(0)
    rayleigh = sums[0, 0] / sums[1, 0]
    total = F32(0.0)
    for c in range(CHUNKS):
        residual = own[c] - rayleigh * trial_rows(c)
        own[c] = residual
        total += jnp.sum(residual * residual)
    sum_term(1, jnp.full((8, 128), total, F32))
    sum_sector(1)
    flush()
    entries = float(sectors * order * order)
    rms_tile = jnp.sqrt(sum_last(1) / entries + 1e-06)
    rms = rms_tile[0, 0]
    ritz_ref[0] = rayleigh
    ritz_ref[1] = rms
    for c in range(CHUNKS):
        vec(1, c)[s, rows(t)] = (own[c] / rms).astype(BF16)
    application(1, lambda: None)
    for c in range(CHUNKS):
        scaled = energy * vec(1, c)[s, rows(t)].astype(F32)
        out_ref[0, :, c * width:(c + 1) * width] = reduce_last(1, c) + scaled
    flush()


def solution(mesh):
    sectors, terms = mesh.shape["sector"], mesh.shape["term"]

    def body(trial_vector, sector_energy, left_blocks, right_blocks, source_sector, coupled):
        count, order = left_blocks.shape[0], left_blocks.shape[2]
        na, nb, nx, share, early = plan(sectors, terms, order)
        width = order // CHUNKS
        sems = 2 * CHUNKS * (nx + 2 * na + 2 * sectors + sectors * nx * 2 + 2 * nx) + 2 * (sectors + terms)
        vmem = pl.BlockSpec(memory_space=pltpu.VMEM)
        smem = pl.BlockSpec(memory_space=pltpu.SMEM)
        hbm = pl.BlockSpec(memory_space=pl.ANY)
        return pl.pallas_call(
            functools.partial(kernel, sectors, terms, count, order),
            out_shape=(
                jax.ShapeDtypeStruct((1, share, order), F32),
                jax.ShapeDtypeStruct((2,), F32),
            ),
            in_specs=[vmem, smem, hbm, hbm, smem, smem],
            out_specs=(vmem, smem),
            scratch_shapes=[
                pltpu.VMEM((count, order, order), BF16),
                pltpu.VMEM((count, order, order), BF16),
                [pltpu.VMEM((sectors, order, width), BF16) for _ in range(2 * CHUNKS)],
                pltpu.VMEM((count, order, order), BF16),
                pltpu.VMEM((CHUNKS, order, width), F32),
                pltpu.VMEM((CHUNKS, nx, share, width), F32),
                pltpu.VMEM((CHUNKS, nx - 1, share, width), F32),
                pltpu.VMEM((CHUNKS, nx - 1, share, width), F32),
                pltpu.VMEM((2, terms, 8, 128), F32),
                pltpu.VMEM((2, sectors, 8, 128), F32),
                pltpu.VMEM((2, 2, 8, 128), F32),
                pltpu.VMEM((CHUNKS, share, width), F32),
                pltpu.SemaphoreType.DMA((sems,)),
                pltpu.SemaphoreType.DMA((sems,)),
                pltpu.SemaphoreType.DMA((count,)),
                pltpu.SemaphoreType.DMA((count,)),
            ],
            compiler_params=pltpu.CompilerParams(
                collective_id=0, has_side_effects=True, vmem_limit_bytes=56 * 1024 * 1024
            ),
        )(trial_vector, sector_energy, left_blocks, right_blocks, source_sector, coupled)

    return jax.shard_map(
        body,
        mesh=mesh,
        in_specs=(
            P("sector", None, None),
            P("sector"),
            P("term", "sector", None, None),
            P("term", "sector", None, None),
            P("term", "sector"),
            P("term", "sector"),
        ),
        out_specs=(P("sector", "term", None), P()),
        check_vma=False,
    )
```

time: 507 us -> 148 us (0.29)
  waiting for transfers between devices: 301 us -> 0 us
  Pallas kernels: 0 us -> 141 us
  other arithmetic: 49 us -> 0 us
  loops' own time: 49 us -> 0 us
  blocking collectives: 39.7 us -> 0 us
  matrix products: 29.4 us -> 0 us
  between operations: 16.5 us -> 1.29 us
  local copies, waits for them, and re-layouts: 19.7 us -> 5.41 us
    all_gather x2 -> x0, waiting for transfers between devices: 150 us -> none  [apply_terms(): whole = lax.all_gather(vector_own, 'sector', axis=0, tiled=True)]
    pallas_call x0 -> x1, Pallas kernels: none -> 141 us  [body(): pl.pallas_call(functools.partial(kernel, sectors, terms, count, order), o...]
    psum x1 -> x0, waiting for transfers between devices: 80.7 us -> none  [body(): first = lax.psum(partial_first, 'term') + energy_col * trial]
    reduce_scatter x1 -> x0, waiting for transfers between devices: 69.5 us -> none  [body(): lax.psum_scatter(partial_second, 'term', scatter_dimension=1, tiled=True)]
    another operation x34 -> x0, loops' own time: 49 us -> none  [the longest x32 27.6 us: step(): lax.cond(coupled[term_idx, sector_idx] > 0, lambda carry: add_block(carry...]
    gt x32 -> x0, other arithmetic: 40.2 us -> none  [step(): coupled[term_idx, sector_idx] > 0]
    psum x2 -> x0, blocking collectives: 39.7 us -> none  [the longest x1 22 us: body(): lax.psum((jnp.sum(trial * first), jnp.sum(trial * trial)), 'sector')]
    dot_general x14 -> x0, matrix products: 29.4 us -> none  [add_block(): jnp.dot(middle, right_blocks[term_idx, sector_idx], preferred_element_typ...]
  transfers between devices with their start and end apart: 4 -> 0, of which waited for: 4 -> 0; matrix products, arithmetic and copies ran while one was open for 0% -> 0% of each run, Pallas kernels for 0% -> 0%
where the time goes in v1:
time: 148 us
  Pallas kernels  141 us (95%)
  local copies, waits for them, and re-layouts  5.41 us (4%)
    pallas_call x1, Pallas kernels, body(): pl.pallas_call(functools.partial(kernel, sectors, terms, count, order), o...  141 us
    unnamed x4, local copies, waits for them, and re-layouts  5.41 us

profile of v1, /device:TPU:0, one launch (start us, length us, event | category | flops | bytes accessed | tf_op | source)
XLA Modules:
  0.0 148.0 jit_solution(7817500642550988094)
XLA Ops:
  1.3 1.3 copy.8.source_ref
  2.6 1.3 copy.9.coupled_ref
  3.9 141.3 %shard_map.77 = (f32[1,128,512]{2,1,0:T(8,128)}, f32[2]{0:T(128)}) custom-call(bf16[1,512,512]{2,1,0:T(8,128)(2,1)} %trial_ref.1, f32[1]{0:T(128)S(6)} %copy.12.energy_ref, bf16[16,1,512,512]{3,2,1,0:T(8,128)(2,1)} %left_hbm.1, bf16[16,1,512,512]{3,2,1,0:T(8,128)(2,1)} %right_hbm.1, s32[16,1]{1,0:T(8,128)} %copy.8.source_ref, s32[16,1]{1,0:T(8,128)} %copy.9.coupled_ref), custom_call_target="tpu_custom_call" | custom-call | tf_op jit(solution)/shard_map/pallas_call | solution.py:326
  145.2 1.7 %copy.13 = f32[1,128,512]{2,1,0:T(8,128)} copy(f32[1,128,512]{2,1,0:T(8,128)} %get-tuple-element.4) | data formatting | bytes 524288
  146.9 1.1 copy.14

commit v2 on v1

--- a/solution.py
+++ b/solution.py
@@ -18,7 +18,7 @@
     nb = sectors // na
     nx = terms // CORES
     share = order // terms
-    early = 48 if (nx == 2 and share == 128) else 0
+    early = 32 if (nx == 2 and share == 128) else 0
     return na, nb, nx, share, early
 
 
@@ -122,6 +122,8 @@
                 push(s, mine, ("c", 0, 0, 0), at_core)
             for i in range(na - 1, 0, -1):
                 push(s, mine, ("a", i), at_a(i))
+            for j in range(1, nb):
+                push(s, mine, ("b", 0, j), at_b(j))
 
         def second():
             if g == 1:
@@ -130,6 +132,8 @@
             if early:
                 for i in range(na - 1, 0, -1):
                     push(s, peer_early, ("aq", i), at_a(i))
+                for j in range(1, nb):
+                    push(s, peer_early, ("bq", 0, j), at_b(j))
             if g == 1:
                 for k in range(1, nx):
                     push(s, rows(quarter(k, core)), ("c", 0, 0, k), at_core)
@@ -140,17 +144,15 @@
             push(sec(i, j), mine, ("c", i, j, 0), at_core)
 
         def third():
-            for i in range(na):
-                if i:
-                    pull(sec(i, 0), mine, ("a", i))
-                    if early:
-                        pull(sec(i, 0), peer_early, ("aq", i))
+            for i in range(1, na):
+                pull(sec(i, 0), mine, ("a", i))
+                if early:
+                    pull(sec(i, 0), peer_early, ("aq", i))
                 for j in range(1, nb):
                     push(sec(i, 0), mine, ("b", i, j), at_b(j))
                     if early:
                         push(sec(i, 0), peer_early, ("bq", i, j), at_b(j))
-                if i:
-                    distribute(i, 0)
+                distribute(i, 0)
 
         def fourth():
             for i in range(na):
@@ -176,24 +178,36 @@
         return [first, second, third, fourth, fifth, last]
 
     def middles(g, c, low, high):
-        def step(k, carry):
-            made = jnp.dot(left[k], vec(g, c)[source_ref[k, 0]], preferred_element_type=F32)
-            mid[k, :, c * width:(c + 1) * width] = jnp.where(coupled_ref[k, 0] > 0, made, 0.0).astype(BF16)
+        def one(k):
+            made = jnp.dot(left[k], vec(g, c)[source_ref[k]], preferred_element_type=F32)
+            mid[k, :, c * width:(c + 1) * width] = jnp.where(coupled_ref[k] > 0, made, 0.0).astype(BF16)
+
+        def step(n, carry):
+            one(low + 2 * n)
+            one(low + 2 * n + 1)
             return carry
 
-        lax.fori_loop(low, high, step, 0)
+        lax.fori_loop(0, (high - low) // 2, step, 0)
 
     def products(c, low, high):
         cols = slice(c * width, (c + 1) * width)
+        group = 4
+
+        def part(k):
+            total = jnp.dot(mid[k], right[k, :, cols], preferred_element_type=F32)
+            for n in range(1, group):
+                total += jnp.dot(mid[k + n], right[k + n, :, cols], preferred_element_type=F32)
+            return total
+
         if low == 0:
-            acc[c] = jnp.dot(mid[0], right[0, :, cols], preferred_element_type=F32)
-            low = 1
-
-        def step(k, carry):
-            acc[c] += jnp.dot(mid[k], right[k, :, cols], preferred_element_type=F32)
+            acc[c] = part(0)
+            low = group
+
+        def step(n, carry):
+            acc[c] += part(low + n * group)
             return carry
 
-        lax.fori_loop(low, high, step, 0)
+        lax.fori_loop(0, (high - low) // group, step, 0)
 
     def reduce_core(g, c):
         for k in range(nx):
@@ -245,19 +259,17 @@
 
     def application(g, between):
         steps = [gather(g, c) for c in range(CHUNKS)]
-        for c in range(CHUNKS):
-            steps[c][0]()
-        for c in range(CHUNKS):
-            steps[c][1]()
-        for stage in range(2, 6):
-            steps[0][stage]()
-        marks = [0, count // 4, half, 3 * count // 4, count]
-        for n in range(4):
-            if g == 0:
-                for k in range(marks[n], marks[n + 1]):
-                    pltpu.make_async_copy(left_hbm.at[k, 0], left.at[k], left_sem.at[k]).wait()
-            middles(g, 0, marks[n], marks[n + 1])
-            steps[1][2 + n]()
+        steps[0][0]()
+        steps[0][1]()
+        for c, stage in ((0, 2), (1, 0), (1, 1), (0, 3), (1, 2), (0, 4), (1, 3), (0, 5)):
+            steps[c][stage]()
+        if g == 0:
+            for k in range(count):
+                pltpu.make_async_copy(left_hbm.at[k, 0], left.at[k], left_sem.at[k]).wait()
+        middles(g, 0, 0, half)
+        steps[1][4]()
+        middles(g, 0, half, count)
+        steps[1][5]()
         middles(g, 1, 0, count)
         if g == 0:
             for k in range(count):
@@ -352,7 +364,7 @@
             compiler_params=pltpu.CompilerParams(
                 collective_id=0, has_side_effects=True, vmem_limit_bytes=56 * 1024 * 1024
             ),
-        )(trial_vector, sector_energy, left_blocks, right_blocks, source_sector, coupled)
+        )(trial_vector, sector_energy, left_blocks, right_blocks, source_sector.reshape(-1), coupled.reshape(-1))
 
     return jax.shard_map(
         body,

time: 148 us -> 111 us (0.75)
  Pallas kernels: 141 us -> 107 us
  local copies, waits for them, and re-layouts: 5.41 us -> 2.8 us
    pallas_call x1, Pallas kernels: 141 us -> 107 us  [body(): pl.pallas_call(functools.partial(kernel, sectors, terms, count, order), o...]
    unnamed x4 -> x2, local copies, waits for them, and re-layouts: 5.41 us -> 2.8 us
where the time goes in v2:
time: 111 us
  Pallas kernels  107 us (96%)
  local copies, waits for them, and re-layouts  2.8 us (3%)
  between operations  1.28 us (1%)
    pallas_call x1, Pallas kernels, body(): pl.pallas_call(functools.partial(kernel, sectors, terms, count, order), o...  107 us
    unnamed x2, local copies, waits for them, and re-layouts  2.8 us

profile of v2, /device:TPU:0, one launch (start us, length us, event | category | flops | bytes accessed | tf_op | source)
XLA Modules:
  0.0 111.2 jit_solution(1371938993088908767)
XLA Ops:
  1.3 107.1 %shard_map.77 = (f32[1,128,512]{2,1,0:T(8,128)}, f32[2]{0:T(128)}) custom-call(bf16[1,512,512]{2,1,0:T(8,128)(2,1)} %trial_ref.1, f32[1]{0:T(128)S(6)} %copy.10.energy_ref, bf16[16,1,512,512]{3,2,1,0:T(8,128)(2,1)} %left_hbm.1, bf16[16,1,512,512]{3,2,1,0:T(8,128)(2,1)} %right_hbm.1, s32[16]{0:T(128)} %bitcast.2, s32[16]{0:T(128)} %bitcast.3), custom_call_target="tpu_custom_call" | custom-call | tf_op jit(solution)/shard_map/pallas_call | solution.py:338
  108.4 1.7 %copy.11 = f32[1,128,512]{2,1,0:T(8,128)} copy(f32[1,128,512]{2,1,0:T(8,128)} %get-tuple-element.4) | data formatting | bytes 524288
  110.1 1.1 %copy.12 = f32[2]{0:T(128)} copy(f32[2]{0:T(128)} %get-tuple-element.5) | data formatting | bytes 16

commit v3 on v2

--- a/solution.py
+++ b/solution.py
@@ -26,7 +26,7 @@
     sectors, terms, count, order,
     trial_ref, energy_ref, left_hbm, right_hbm, source_ref, coupled_ref,
     out_ref, ritz_ref,
-    left, right, vecs, mid, acc, rs_core, rs_send, rs_x, red_term, red_sector, red_send, own,
+    left, right, vecs, mid, acc, rs_core, rs_send, rs_x, rs_send2, rs_x2, red_term, red_sector, red_send, own,
     send_sem, recv_sem, left_sem, right_sem,
 ):
     na, nb, nx, share, early = plan(sectors, terms, order)
@@ -218,15 +218,17 @@
         for k in range(1, nx):
             recv(rs_core.at[c, k], ("rc", g, c, k))
             part = lax.rem(x + k, nx) * CORES + core
-            rs_send[c, k - 1] = acc[c, rows(part)] + rs_core[c, k]
-            send(rs_send.at[c, k - 1], rs_x.at[c, k - 1], ("rx", g, c, k), at_x(k))
+            out, into = (rs_send2, rs_x2) if g else (rs_send, rs_x)
+            out[c, k - 1] = (acc[c, rows(part)] + rs_core[c, k]).astype(out.dtype)
+            send(out.at[c, k - 1], into.at[c, k - 1], ("rx", g, c, k), at_x(k))
 
     def reduce_last(g, c):
         recv(rs_core.at[c, 0], ("rc", g, c, 0))
         total = acc[c, rows(t)] + rs_core[c, 0]
         for k in range(1, nx):
-            recv(rs_x.at[c, k - 1], ("rx", g, c, k))
-            total = total + rs_x[c, k - 1]
+            into = rs_x2 if g else rs_x
+            recv(into.at[c, k - 1], ("rx", g, c, k))
+            total = total + into[c, k - 1].astype(F32)
         return total
 
     def sum_term(n, tile):
@@ -352,6 +354,8 @@
                 pltpu.VMEM((CHUNKS, nx, share, width), F32),
                 pltpu.VMEM((CHUNKS, nx - 1, share, width), F32),
                 pltpu.VMEM((CHUNKS, nx - 1, share, width), F32),
+                pltpu.VMEM((CHUNKS, nx - 1, share, width), BF16),
+                pltpu.VMEM((CHUNKS, nx - 1, share, width), BF16),
                 pltpu.VMEM((2, terms, 8, 128), F32),
                 pltpu.VMEM((2, sectors, 8, 128), F32),
                 pltpu.VMEM((2, 2, 8, 128), F32),

time: 111 us -> 110 us (level)
    pallas_call x1, Pallas kernels: 107 us -> 106 us  [body(): pl.pallas_call(functools.partial(kernel, sectors, terms, count, order), o...]
where the time goes in v3:
time: 110 us
  Pallas kernels  106 us (96%)
  local copies, waits for them, and re-layouts  2.8 us (3%)
  between operations  1.28 us (1%)
    pallas_call x1, Pallas kernels, body(): pl.pallas_call(functools.partial(kernel, sectors, terms, count, order), o...  106 us
    unnamed x2, local copies, waits for them, and re-layouts  2.8 us

profile of v3, /device:TPU:0, one launch (start us, length us, event | category | flops | bytes accessed | tf_op | source)
XLA Modules:
  0.0 109.7 jit_solution(5641383901278080249)
XLA Ops:
  1.3 105.6 %shard_map.77 = (f32[1,128,512]{2,1,0:T(8,128)}, f32[2]{0:T(128)}) custom-call(bf16[1,512,512]{2,1,0:T(8,128)(2,1)} %trial_ref.1, f32[1]{0:T(128)S(6)} %copy.10.energy_ref, bf16[16,1,512,512]{3,2,1,0:T(8,128)(2,1)} %left_hbm.1, bf16[16,1,512,512]{3,2,1,0:T(8,128)(2,1)} %right_hbm.1, s32[16]{0:T(128)} %bitcast.2, s32[16]{0:T(128)} %bitcast.3), custom_call_target="tpu_custom_call" | custom-call | tf_op jit(solution)/shard_map/pallas_call | solution.py:340
  106.9 1.7 %copy.11 = f32[1,128,512]{2,1,0:T(8,128)} copy(f32[1,128,512]{2,1,0:T(8,128)} %get-tuple-element.4) | data formatting | bytes 524288
  108.5 1.1 %copy.12 = f32[2]{0:T(128)} copy(f32[2]{0:T(128)} %get-tuple-element.5) | data formatting | bytes 16
